TPU v7x, 32 devices: a whole 2x2x4 slice. The times are simulated.
32 devices in a mesh: dp: 4 (over y, x), tensor: 8 (over z, core).
Axes of the slice: x: 2, y: 2, z: 4, core: 2. Of those that a mesh axis runs over, the one named last changes fastest.
Arguments:
- block_in: bfloat16 [8192, 1024], P(('dp', 'tensor')), may hold values from -10 to 10
- cotangent: bfloat16 [8192, 1024], P(('dp', 'tensor')), may hold values from -6 to 6
- lengths: int32 [16], P('dp'), may hold values from 1 to 512, as said below
- qkv_weight: float32 [3, 1024, 1024], P(None, 'dp', 'tensor'), may hold values from -0.1875 to 0.1875
- proj_weight: float32 [1024, 1024], P('tensor', 'dp'), may hold values from -0.75 to 0.75
- expand_weight: float32 [1024, 4096], P('dp', 'tensor'), may hold values from -0.1875 to 0.1875
- reduce_weight: float32 [4096, 1024], P('tensor', 'dp'), may hold values from -0.09375 to 0.09375
- split_bias: float32 [16, 384], P('tensor', 'dp'), may hold values from -0.6 to 0.6
- vector_params: float32 [6, 1024], P(None, 'dp'), may hold values from -0.6 to 0.6
- qkv_moments: float32 [2, 3, 1024, 1024], P(None, None, 'dp', 'tensor'), may hold values from -3 to 3, as said below
- proj_moments: float32 [2, 1024, 1024], P(None, 'tensor', 'dp'), may hold values from -3 to 3, as said below
- expand_moments: float32 [2, 1024, 4096], P(None, 'dp', 'tensor'), may hold values from -3 to 3, as said below
- reduce_moments: float32 [2, 4096, 1024], P(None, 'tensor', 'dp'), may hold values from -3 to 3, as said below
- bias_moments: float32 [2, 16, 384], P(None, 'tensor', 'dp'), may hold values from -3 to 3, as said below
- vector_moments: float32 [2, 6, 1024], P(None, None, 'dp'), may hold values from -3 to 3, as said below
Outputs:
- block_out: bfloat16 [8192, 1024], P(('dp', 'tensor'))
- input_grad: bfloat16 [8192, 1024], P(('dp', 'tensor'))
- qkv_grad: float32 [3, 1024, 1024], P(None, 'dp', 'tensor')
- proj_grad: float32 [1024, 1024], P('tensor', 'dp')
- expand_grad: float32 [1024, 4096], P('dp', 'tensor')
- reduce_grad: float32 [4096, 1024], P('tensor', 'dp')
- bias_grad: float32 [16, 384], P('tensor', 'dp')
- vector_grad: float32 [6, 1024], P(None, 'dp')
- qkv_new: float32 [3, 1024, 1024], P(None, 'dp', 'tensor')
- proj_new: float32 [1024, 1024], P('tensor', 'dp')
- expand_new: float32 [1024, 4096], P('dp', 'tensor')
- reduce_new: float32 [4096, 1024], P('tensor', 'dp')
- bias_new: float32 [16, 384], P('tensor', 'dp')
- vector_new: float32 [6, 1024], P(None, 'dp')
- qkv_state: float32 [2, 3, 1024, 1024], P(None, None, 'dp', 'tensor')
- proj_state: float32 [2, 1024, 1024], P(None, 'tensor', 'dp')
- expand_state: float32 [2, 1024, 4096], P(None, 'dp', 'tensor')
- reduce_state: float32 [2, 4096, 1024], P(None, 'tensor', 'dp')
- bias_state: float32 [2, 16, 384], P(None, 'tensor', 'dp')
- vector_state: float32 [2, 6, 1024], P(None, None, 'dp')
Inputs may be any that keep to these rules, and one draw needn't show every extreme that they name: `lengths`: sequence s lies on the dp member s // (number of sequences per dp member); every draw has a sequence of exactly 512 live slots. `qkv_moments`: index 0 holds first moments, index 1 second moments of at least 0.01. `proj_moments`: index 0 holds first moments, index 1 second moments of at least 0.01. `expand_moments`: index 0 holds first moments, index 1 second moments of at least 0.01. `reduce_moments`: index 0 holds first moments, index 1 second moments of at least 0.01. `bias_moments`: index 0 holds first moments, index 1 second moments of at least 0.01. `vector_moments`: index 0 holds first moments, index 1 second moments of at least 0.01.
All inputs are finite; a program needn't handle non-finite values.
Results may differ from a plain program's by a relative error of at most 0.025.
Values may be sent and summed in bfloat16 or wider, within the bound.
No kernel may reach another device: no remote copies, remote signals or barrier semaphores. Data moves between devices by JAX's collectives and lax.ppermute only.
A program may use at most 192 MiB of HBM per device.

v0:
```python
import jax
import jax.numpy as jnp
from jax import lax
from jax.sharding import PartitionSpec as P

L = 512
SEQS_DEV = 4
STEP = 10
HD = 64
norm_eps = 1e-05
beta_one = 0.9
beta_two = 0.999
learn_rate = 0.02
decay_rate = 0.01
adam_eps = 1e-08


def layer_norm(resid, gain, shift):
    center = resid - jnp.mean(resid, axis=-1, keepdims=True)
    inv_std = lax.rsqrt(jnp.mean(center * center, axis=-1, keepdims=True) + norm_eps)
    normed = center * inv_std
    return (normed * (1.0 + gain) + shift, normed, inv_std)


def norm_back(upstream, normed, inv_std, gain):
    scaled = upstream * (1.0 + gain)
    return inv_std * (
        scaled
        - jnp.mean(scaled, axis=-1, keepdims=True)
        - normed * jnp.mean(scaled * normed, axis=-1, keepdims=True)
    )


def gelu_pair(before):
    cumul = 0.5 * (1.0 + lax.erf(before * 0.7071067811865476))
    density = jnp.exp(-0.5 * before * before) * 0.3989422804014327
    return (before * cumul, cumul + before * density)


def adamw_step(weight, moments, grad, decay):
    first = beta_one * moments[0] + (1.0 - beta_one) * grad
    second = beta_two * moments[1] + (1.0 - beta_two) * grad * grad
    scale_one = 1.0 - beta_one**STEP
    scale_two = 1.0 - beta_two**STEP
    update = first / scale_one / (jnp.sqrt(second / scale_two) + adam_eps) + decay * weight
    return (weight - learn_rate * update, jnp.stack([first, second]))


def live_rows(lengths, count):
    positions = jnp.arange(count, dtype=jnp.int32)
    slot_ids = jnp.arange(lengths.shape[0], dtype=jnp.int32)
    chosen = (positions // L)[:, None] == slot_ids[None, :]
    row_length = jnp.sum(jnp.where(chosen, lengths[None, :], 0), axis=1)
    return positions % L < row_length


def spread(rows_b):
    return lax.all_gather(rows_b, "tensor", axis=0, tiled=True)


def split_heads(matrix, heads_dev):
    return matrix.reshape(SEQS_DEV, L, heads_dev, HD)


def head_scores(query_h, keys_h, key_mask):
    raw = jnp.einsum(
        "sqhe,skhe->shqk", query_h, keys_h, preferred_element_type=jnp.float32
    ) * HD ** (-0.5)
    return jnp.where(key_mask, raw, -jnp.inf)


def on_device(
    block_in,
    cotangent,
    lengths,
    qkv_weight,
    proj_weight,
    expand_weight,
    reduce_weight,
    split_bias,
    vector_params,
    qkv_moments,
    proj_moments,
    expand_moments,
    reduce_moments,
    bias_moments,
    vector_moments,
):
    half = jnp.bfloat16
    single = jnp.float32
    qkv_w, proj_w, expand_w, reduce_w, bias_w, vector_w = (
        lax.all_gather(qkv_weight.astype(half), "dp", axis=1, tiled=True),
        lax.all_gather(proj_weight.astype(half), "dp", axis=1, tiled=True),
        lax.all_gather(expand_weight.astype(half), "dp", axis=0, tiled=True),
        lax.all_gather(reduce_weight.astype(half), "dp", axis=1, tiled=True),
        lax.all_gather(split_bias.astype(half), "dp", axis=1, tiled=True),
        lax.all_gather(vector_params.astype(half), "dp", axis=1, tiled=True),
    )
    heads_dev = bias_w.shape[0]
    width = heads_dev * HD
    bias_f = bias_w.astype(single)
    query_bias = bias_f[:, :HD].reshape(width)
    value_bias = bias_f[:, HD : 2 * HD].reshape(width)
    hidden_bias = bias_f[:, 2 * HD :].reshape(-1)
    vectors = vector_w.astype(single)
    share = block_in.shape[0]
    total_rows = share * lax.axis_size("tensor")
    first_row = lax.axis_index("tensor") * share
    live_full = live_rows(lengths, total_rows)
    key_mask = live_full.reshape(SEQS_DEV, 1, 1, L)
    x_full = spread(block_in)

    def reduce_rows(term):
        return lax.psum(term.astype(jnp.bfloat16), "tensor").astype(jnp.float32)

    def own_rows(matrix):
        return lax.dynamic_slice_in_dim(matrix, first_row, share, 0)

    projected = jnp.einsum("td,jde->jte", x_full, qkv_w, preferred_element_type=single)
    query = (projected[0] + query_bias).astype(half)
    keys = projected[1].astype(half)
    values = (projected[2] + value_bias).astype(half)
    query_h = split_heads(query, heads_dev)
    keys_h = split_heads(keys, heads_dev)
    values_h = split_heads(values, heads_dev)
    scores = head_scores(query_h, keys_h, key_mask)
    row_max = jnp.max(scores, axis=-1, keepdims=True)
    exponent = jnp.exp(scores - row_max)
    denominator = jnp.sum(exponent, axis=-1, keepdims=True)
    log_total = row_max + jnp.log(denominator)
    weights_b = (exponent / denominator).astype(half)
    heads_out = jnp.einsum("shqk,skhe->sqhe", weights_b, values_h, preferred_element_type=single)
    heads_out = heads_out.astype(half).reshape(total_rows, width)
    attn_term = jnp.dot(heads_out, proj_w, preferred_element_type=single)
    resid_one = x_full.astype(single) + reduce_rows(attn_term) + vectors[0]
    hidden_f, normed_one, inv_one = layer_norm(resid_one, vectors[1], vectors[2])
    hidden_b = hidden_f.astype(half)
    before = jnp.dot(hidden_b, expand_w, preferred_element_type=single) + hidden_bias
    active, slope = gelu_pair(before)
    active_b = active.astype(half)
    ffn_term = jnp.dot(active_b, reduce_w, preferred_element_type=single)
    resid_two = hidden_f + reduce_rows(ffn_term) + vectors[3]
    out_f, normed_two, inv_two = layer_norm(resid_two, vectors[4], vectors[5])
    block_out = own_rows(out_f).astype(half)
    grad_out = jnp.where(live_full[:, None], spread(cotangent).astype(single), 0.0)
    d_two = norm_back(grad_out, normed_two, inv_two, vectors[4])
    d_two_b = d_two.astype(half)
    g_reduce = jnp.einsum("tf,td->fd", active_b, d_two_b, preferred_element_type=single)
    d_pre = jnp.einsum("td,fd->tf", d_two_b, reduce_w, preferred_element_type=single) * slope
    g_hidden_bias = jnp.sum(d_pre, axis=0)
    d_pre_b = d_pre.astype(half)
    g_expand = jnp.einsum("td,tf->df", hidden_b, d_pre_b, preferred_element_type=single)
    hidden_term = jnp.einsum("tf,df->td", d_pre_b, expand_w, preferred_element_type=single)
    d_hidden = d_two + reduce_rows(hidden_term)
    d_one = norm_back(d_hidden, normed_one, inv_one, vectors[1])
    vector_parts = jnp.stack(
        [
            jnp.sum(d_one, axis=0),
            jnp.sum(d_hidden * normed_one, axis=0),
            jnp.sum(d_hidden, axis=0),
            jnp.sum(d_two, axis=0),
            jnp.sum(grad_out * normed_two, axis=0),
            jnp.sum(grad_out, axis=0),
        ]
    )
    d_one_b = d_one.astype(half)
    g_proj = jnp.einsum("te,td->ed", heads_out, d_one_b, preferred_element_type=single)
    d_heads = jnp.einsum("td,ed->te", d_one_b, proj_w, preferred_element_type=single).astype(half)
    d_heads_h = split_heads(d_heads, heads_dev)
    back_prob = jnp.exp(head_scores(query_h, keys_h, key_mask) - log_total)
    d_prob = jnp.einsum("sqhe,skhe->shqk", d_heads_h, values_h, preferred_element_type=single)
    delta = jnp.sum(back_prob * d_prob, axis=-1, keepdims=True)
    d_score = (back_prob * (d_prob - delta) * HD ** (-0.5)).astype(half)
    back_b = back_prob.astype(half)
    d_query = jnp.einsum("shqk,skhe->sqhe", d_score, keys_h, preferred_element_type=single)
    d_keys = jnp.einsum("shqk,sqhe->skhe", d_score, query_h, preferred_element_type=single)
    d_values = jnp.einsum("shqk,sqhe->skhe", back_b, d_heads_h, preferred_element_type=single)
    d_query = d_query.reshape(total_rows, width)
    d_keys = d_keys.reshape(total_rows, width)
    d_values = d_values.reshape(total_rows, width)
    d_stack = jnp.stack([d_query, d_keys, d_values]).astype(half)
    g_qkv = jnp.einsum("td,jte->jde", x_full, d_stack, preferred_element_type=single)
    input_term = jnp.einsum("jte,jde->td", d_stack, qkv_w, preferred_element_type=single)
    input_grad = own_rows(d_one + reduce_rows(input_term)).astype(half)
    g_split = jnp.concatenate(
        [
            jnp.sum(d_query, axis=0).reshape(heads_dev, HD),
            jnp.sum(d_values, axis=0).reshape(heads_dev, HD),
            g_hidden_bias.reshape(heads_dev, -1),
        ],
        axis=1,
    )
    qkv_sum, proj_sum, expand_sum, reduce_sum, bias_sum, vector_sum = (
        lax.psum_scatter(g_qkv, "dp", scatter_dimension=1, tiled=True),
        lax.psum_scatter(g_proj, "dp", scatter_dimension=1, tiled=True),
        lax.psum_scatter(g_expand, "dp", scatter_dimension=0, tiled=True),
        lax.psum_scatter(g_reduce, "dp", scatter_dimension=1, tiled=True),
        lax.psum_scatter(g_split, "dp", scatter_dimension=1, tiled=True),
        lax.psum_scatter(vector_parts, "dp", scatter_dimension=1, tiled=True),
    )
    qkv_new, qkv_state = adamw_step(qkv_weight, qkv_moments, qkv_sum, decay_rate)
    proj_new, proj_state = adamw_step(proj_weight, proj_moments, proj_sum, decay_rate)
    expand_new, expand_state = adamw_step(expand_weight, expand_moments, expand_sum, decay_rate)
    reduce_new, reduce_state = adamw_step(reduce_weight, reduce_moments, reduce_sum, decay_rate)
    bias_new, bias_state = adamw_step(split_bias, bias_moments, bias_sum, 0.0)
    vector_new, vector_state = adamw_step(vector_params, vector_moments, vector_sum, 0.0)
    return (
        block_out,
        input_grad,
        qkv_sum,
        proj_sum,
        expand_sum,
        reduce_sum,
        bias_sum,
        vector_sum,
        qkv_new,
        proj_new,
        expand_new,
        reduce_new,
        bias_new,
        vector_new,
        qkv_state,
        proj_state,
        expand_state,
        reduce_state,
        bias_state,
        vector_state,
    )


def solution(mesh):
    placed = (
        P(("dp", "tensor"), None),
        P(("dp", "tensor"), None),
        P("dp"),
        P(None, "dp", "tensor"),
        P("tensor", "dp"),
        P("dp", "tensor"),
        P("tensor", "dp"),
        P("tensor", "dp"),
        P(None, "dp"),
        P(None, None, "dp", "tensor"),
        P(None, "tensor", "dp"),
        P(None, "dp", "tensor"),
        P(None, "tensor", "dp"),
        P(None, "tensor", "dp"),
        P(None, None, "dp"),
    )
    return jax.shard_map(
        on_device,
        mesh=mesh,
        in_specs=placed,
        out_specs=(
            P(("dp", "tensor"), None),
            P(("dp", "tensor"), None),
            P(None, "dp", "tensor"),
            P("tensor", "dp"),
            P("dp", "tensor"),
            P("tensor", "dp"),
            P("tensor", "dp"),
            P(None, "dp"),
            P(None, "dp", "tensor"),
            P("tensor", "dp"),
            P("dp", "tensor"),
            P("tensor", "dp"),
            P("tensor", "dp"),
            P(None, "dp"),
            P(None, None, "dp", "tensor"),
            P(None, "tensor", "dp"),
            P(None, "dp", "tensor"),
            P(None, "tensor", "dp"),
            P(None, "tensor", "dp"),
            P(None, None, "dp"),
        ),
        check_vma=False,
    )
```

profile of v0, /device:TPU:0, one launch (start us, length us, event | category | flops | bytes accessed | tf_op | source)
XLA Modules:
  0.0 728.4 jit_solution(12276453182244348398)
XLA Ops:
  9.5 9.4 %all-gather = bf16[4,96,2]{1,2,0:T(2,128)(2,1)S(1)} all-gather(bf16[1,96,2]{1,2,0:T(2,128)(2,1)S(1)} %convert_bitcast_fusion), channel_id=1, replica_groups=mesh['dp'=4,'tensor'=8] {'dp'}, dimensions={0}, use_global_device_ids=true | all-gather | bytes 1920 | tf_op jit(solution)/shard_map/all_gather | solution.py:96
  22.1 10.0 %all_gather.27 = bf16[128,1024]{1,0:T(8,128)(2,1)S(1)} all-gather(bf16[128,256]{1,0:T(8,128)(2,1)S(1)} %convert_element_type.117), channel_id=1, replica_groups=mesh['dp'=4,'tensor'=8] {'dp'}, dimensions={1}, use_global_device_ids=true | all-gather | bytes 327680 | tf_op jit(solution)/shard_map/all_gather | solution.py:93
  32.0 13.3 %all_gather.25 = bf16[3,1024,128]{1,2,0:T(8,128)(2,1)S(1)} all-gather(bf16[3,256,128]{1,2,0:T(8,128)(2,1)S(1)} %convert_element_type.108), channel_id=1, replica_groups=mesh['dp'=4,'tensor'=8] {'dp'}, dimensions={1}, use_global_device_ids=true | all-gather | bytes 983040 | tf_op jit(solution)/shard_map/all_gather | solution.py:92
  45.4 14.6 %all-gather.6.cloned.1.call-done = bf16[2048,1024]{1,0:T(8,128)(2,1)} async-done(((bf16[256,1024]{1,0:T(8,128)(2,1)}), bf16[2048,1024]{1,0:T(8,128)(2,1)}) %all-gather.6.cloned.1.call-update) | async-done | bytes 4194320 | tf_op jit(solution)/shard_map/all_gather | solution.py:58
  81.2 8.7 %all_gather.28 = bf16[6,1024]{1,0:T(8,128)(2,1)S(1)} all-gather(bf16[6,256]{1,0:T(8,128)(2,1)S(1)} %convert_element_type.120), channel_id=1, replica_groups=mesh['dp'=4,'tensor'=8] {'dp'}, dimensions={1}, use_global_device_ids=true | all-gather | bytes 15360 | tf_op jit(solution)/shard_map/all_gather | solution.py:97
  90.0 85.0 %all-reduce.5.cloned.1.call-done = bf16[2048,1024]{1,0:T(8,128)(2,1)} async-done(((bf16[2048,1024]{1,0:T(8,128)(2,1)}), bf16[2048,1024]{1,0:T(8,128)(2,1)}) %all-reduce.5.cloned.1.call-update) | async-done | bytes 4194320 | tf_op jit(solution)/shard_map/psum | solution.py:114
  183.1 7.5 %multiply_convert_fusion.1 = (bf16[2048,512]{1,0:T(8,128)(2,1)}, f32[2048,512]{1,0:T(8,128)}) fusion(f32[512]{0:T(512)S(1)} %bitcast.225, bf16[1024,512]{1,0:T(8,128)(2,1)} %all-gather.8.cloned.1.call-done, f32[1024]{0:T(1024)S(1)} %bitcast.203, f32[1024]{0:T(1024)S(1)} %bitcast.192, f32[2048]{0:T(1024)S(1)} %add_rsqrt_fusion.1, ...), kind=kOutput, calls=%fused_computation.46 | convolution fusion | flops 2172649472 | bytes 15759360 | tf_op jit(solution)/shard_map/dot_general | solution.py:138
  190.6 6.1 convolution_convert_fusion.1
  197.5 95.9 %all-reduce.7.cloned.1.call-done = bf16[2048,1024]{1,0:T(8,128)(2,1)} async-done(((bf16[2048,1024]{1,0:T(8,128)(2,1)}), bf16[2048,1024]{1,0:T(8,128)(2,1)}) %all-reduce.7.cloned.1.call-update) | async-done | bytes 4194320 | tf_op jit(solution)/shard_map/psum | solution.py:114
  293.4 7.9 %fusion.74 = f32[2048]{0:T(1024)S(1)} fusion(f32[1024]{0:T(1024)S(1)} %bitcast.208, bf16[2048,1024]{1,0:T(8,128)(2,1)} %all-reduce.7.cloned.1.call-done, f32[1024]{0:T(1024)S(1)} %bitcast.204, f32[1024]{0:T(1024)S(1)} %bitcast.193, f32[2048]{0:T(1024)S(1)} %add_rsqrt_fusion.1, f32[2048]{0:T(1024)S(1)} %broadcast_multiply_fusion.5, f32[1024]{0:T(1024)S(1)} %bitcast.186, ...), kind=kLoop, calls=%fused_computation.102 | loop fusion | flops 25163776 | bytes 12623872 | tf_op jit(solution)/shard_map/reduce_sum | solution.py:19
  306.8 35.0 %all-gather.12.cloned.1.call-done = bf16[2048,1024]{1,0:T(8,128)(2,1)} async-done(((bf16[256,1024]{1,0:T(8,128)(2,1)}), bf16[2048,1024]{1,0:T(8,128)(2,1)}) %all-gather.12.cloned.1.call-update) | async-done | bytes 4194320 | tf_op jit(solution)/shard_map/all_gather | solution.py:58
  341.8 11.6 %multiply_reduce_fusion = (f32[1024]{0:T(1024)S(1)}, f32[2048]{0:T(1024)S(1)}, f32[2048]{0:T(1024)S(1)}, f32[1024]{0:T(1024)S(1)}, f32[2048,1024]{1,0:T(8,128)S(1)}) fusion(bf16[2048,1024]{1,0:T(8,128)(2,1)} %all-gather.12.cloned.1.call-done, pred[2048]{0:T(1024)(128)(4,1)S(1)} %fusion.98, f32[1024]{0:T(1024)S(1)} %bitcast.200, f32[2048]{0:T(1024)S(1)} %add_rsqrt_fusion, ...), kind=kLoop, calls=%fused_computation.2 | loop fusion | flops 46131200 | bytes 25245696 | tf_op jit(solution)/shard_map/reduce_sum | solution.py:162
  370.0 95.1 %all-reduce.9.cloned.1.call-done = bf16[2048,1024]{1,0:T(8,128)(2,1)} async-done(((bf16[2048,1024]{1,0:T(8,128)(2,1)}), bf16[2048,1024]{1,0:T(8,128)(2,1)}) %all-reduce.9.cloned.1.call-update) | async-done | bytes 4194320 | tf_op jit(solution)/shard_map/psum | solution.py:114
  465.1 12.0 %multiply_reduce_fusion.1 = (f32[1024]{0:T(1024)S(1)}, f32[2048]{0:T(1024)S(1)}, f32[2048]{0:T(1024)S(1)}, f32[1024]{0:T(1024)S(1)}, f32[1024]{0:T(1024)S(1)}) fusion(f32[2048,1024]{1,0:T(8,128)} %copy-done.7, bf16[2048,1024]{1,0:T(8,128)(2,1)} %all-reduce.9.cloned.1.call-done, f32[2048]{0:T(1024)S(1)} %add_rsqrt_fusion.1, ...), kind=kLoop, calls=%fused_computation.3 | loop fusion | flops 33547264 | bytes 21024768 | tf_op jit(solution)/shard_map/reduce_sum | solution.py:159
  477.2 6.6 fusion.123
  499.4 6.2 fusion.126
  505.7 16.0 %fusion.125 = (f32[2,64]{1,0:T(2,128)S(1)}, bf16[4,512,2,64]{1,3,2,0:T(8,128)(2,1)S(1)}) fusion(f32[4,2,512,512]{2,3,1,0:T(8,128)} %fusion.77, f32[4,2,512]{2,1,0:T(2,128)S(1)} %bitcast.223, f32[4,2,512,512]{2,3,1,0:T(8,128)} %copy-done.8, pred[4,512]{1,0:T(4,128)(4,1)S(1)} %fusion.96, bf16[4,512,2,64]{1,0,3,2:T(4,128)(2,1)S(1)} %convert_element_type.113), kind=kOutput, calls=%fused_computation.184 | convolution fusion | flops 292032896 | bytes 17844736 | tf_op jit(solution)/shard_map/shqk,skhe->sqhe/dot_general | solution.py:175
  528.2 15.8 %fusion.53 = bf16[4,512,2,64]{1,3,2,0:T(8,128)(2,1)S(1)} fusion(f32[4,2,512,512]{2,3,1,0:T(8,128)} %fusion.77, f32[4,2,512]{2,1,0:T(2,128)S(1)} %bitcast.224, f32[4,2,512,512]{2,3,1,0:T(8,128)} %copy-done.8, pred[4,512]{1,0:T(4,128)(4,1)S(1)} %fusion.96, f32[4,512,2,64]{1,0,3,2:T(4,128)S(1)} %squeeze.5, f32[2,64]{1,0:T(2,128)S(1)} %get-tuple-element.167), kind=kOutput, calls=%fused_computation.67 | convolution fusion | flops 292295168 | bytes 18369024 | tf_op jit(solution)/shard_map/shqk,sqhe->skhe/dot_general | solution.py:176
  553.1 8.6 %fusion.57 = f32[1024,512]{1,0:T(8,128)} fusion(f32[1024]{0:T(1024)S(1)} %bitcast.207, f32[1024]{0:T(1024)S(1)} %bitcast.198, bf16[2048,512]{1,0:T(8,128)(2,1)} %copy-done.34, bf16[2048,1024]{1,0:T(8,128)(2,1)} %all-reduce.5.cloned.1.call-done, bf16[2048,1024]{1,0:T(8,128)(2,1)} %all-gather.6.cloned.1.call-done, f32[2048]{0:T(1024)S(1)} %add_rsqrt_fusion.1, ...), kind=kOutput, calls=%fused_computation.69 | convolution fusion | flops 2166358016 | bytes 12611584 | tf_op jit(solution)/shard_map/td,tf->df/dot_general | solution.py:152
  562.1 7.8 %fusion.37 = f32[512,1024]{1,0:T(8,128)} fusion(bf16[2048,512]{1,0:T(8,128)(2,1)} %get-tuple-element.170, f32[2048,1024]{1,0:T(8,128)} %copy-done.7), kind=kOutput, calls=%fused_computation.59 | convolution fusion | flops 2149580800 | bytes 12582912 | tf_op jit(solution)/shard_map/tf,td->fd/dot_general | solution.py:148
  582.0 22.0 %reduce-scatter.11.cloned.1.call-done = f32[128,256]{1,0:T(8,128)} async-done(((f32[128,1024]{1,0:T(8,128)}), f32[128,256]{1,0:T(8,128)}) %reduce-scatter.11.cloned.1.call-update) | async-done | bytes 131088 | tf_op jit(solution)/shard_map/reduce_scatter | solution.py:195
  606.4 43.4 %all-reduce.11.cloned.1.call-done = bf16[2048,1024]{1,0:T(8,128)(2,1)} async-done(((bf16[2048,1024]{1,0:T(8,128)(2,1)}), bf16[2048,1024]{1,0:T(8,128)(2,1)}) %all-reduce.11.cloned.1.call-update) | async-done | bytes 4194320 | tf_op jit(solution)/shard_map/psum | solution.py:114
  655.9 25.3 %reduce-scatter.15.cloned.1.call-done = f32[512,256]{1,0:T(8,128)} async-done(((f32[512,1024]{1,0:T(8,128)}), f32[512,256]{1,0:T(8,128)}) %reduce-scatter.15.cloned.1.call-update) | async-done | bytes 524304 | tf_op jit(solution)/shard_map/reduce_scatter | solution.py:197
  684.8 30.3 %reduce-scatter.9.cloned.1.call-done = f32[3,256,128]{1,2,0:T(8,128)} async-done(((f32[3,1024,128]{1,2,0:T(8,128)}), f32[3,256,128]{1,2,0:T(8,128)}) %reduce-scatter.9.cloned.1.call-update) | async-done | bytes 393232 | tf_op jit(solution)/shard_map/reduce_scatter | solution.py:194
  (192 shorter events, 117.6 us)
Async XLA Ops:
  8.0 52.0 %all-gather.6.cloned.1.call-start = ((), (), s32[]{:S(2)}) async-start(), calls=%async_computation.6 | async-start | bytes 4718592 | tf_op jit(solution)/shard_map/all_gather | solution.py:58
  8.8 166.2 %all-reduce.5.cloned.1.call-start = ((), (), s32[]{:S(2)}) async-start(), calls=%async_computation.7 | async-start | bytes 8388608 | tf_op jit(solution)/shard_map/psum | solution.py:114
  21.0 44.3 %copy-start.14 = (f32[3,256,128]{1,2,0:T(8,128)}, f32[3,256,128]{1,2,0:T(8,128)S(1)}, u32[]{:S(2)}) copy-start(f32[3,256,128]{1,2,0:T(8,128)S(1)} %copy.154) | copy-start | bytes 1179652
  45.3 14.7 %copy-start.22 = (bf16[3,1024,128]{1,2,0:T(8,128)(2,1)}, bf16[3,1024,128]{1,2,0:T(8,128)(2,1)S(1)}, u32[]{:S(2)}) copy-start(bf16[3,1024,128]{1,2,0:T(8,128)(2,1)S(1)} %all_gather.25) | copy-start | bytes 2359300
  79.5 103.5 %all-gather.8.cloned.1.call-start = ((), (), s32[]{:S(2)}) async-start(), calls=%async_computation.8 | async-start | bytes 1310720 | tf_op jit(solution)/shard_map/all_gather | solution.py:94
  80.4 110.2 %all-gather.10.cloned.1.call-start = ((), (), s32[]{:S(2)}) async-start(), calls=%async_computation.9 | async-start | bytes 1310720 | tf_op jit(solution)/shard_map/all_gather | solution.py:95
  81.2 212.2 %all-reduce.7.cloned.1.call-start = ((), (), s32[]{:S(2)}) async-start(), calls=%async_computation.10 | async-start | bytes 8388608 | tf_op jit(solution)/shard_map/psum | solution.py:114
  196.7 145.1 %all-gather.12.cloned.1.call-start = ((), (), s32[]{:S(2)}) async-start(), calls=%async_computation.11 | async-start | bytes 4718592 | tf_op jit(solution)/shard_map/all_gather | solution.py:58
  197.3 267.8 %all-reduce.9.cloned.1.call-start = ((), (), s32[]{:S(2)}) async-start(), calls=%async_computation.12 | async-start | bytes 8388608 | tf_op jit(solution)/shard_map/psum | solution.py:114
  369.7 208.3 %reduce-scatter.19.cloned.1.call-start = ((), (), s32[]{:S(2)}) async-start(), calls=%async_computation.19 | async-start | bytes 245760
  465.1 12.0 %copy-start.12 = (bf16[2048,1024]{1,0:T(8,128)(2,1)S(1)}, bf16[2048,1024]{1,0:T(8,128)(2,1)}, u32[]{:S(2)}) copy-start(bf16[2048,1024]{1,0:T(8,128)(2,1)} %all-reduce.9.cloned.1.call-done) | copy-start | bytes 12582916
  522.6 57.5 %reduce-scatter.17.cloned.1.call-start = ((), (), s32[]{:S(2)}) async-start(), calls=%async_computation.18 | async-start | bytes 40960 | tf_op jit(solution)/shard_map/reduce_scatter | solution.py:199
  528.2 18.4 %copy-start.23 = (bf16[4,512,2,64]{1,3,2,0:T(8,128)(2,1)S(1)}, bf16[4,512,2,64]{1,3,2,0:T(8,128)(2,1)}, u32[]{:S(2)}) copy-start(bf16[4,512,2,64]{1,3,2,0:T(8,128)(2,1)} %get-tuple-element.143) | copy-start | bytes 1572868
  528.2 75.8 %reduce-scatter.11.cloned.1.call-start = ((), (), s32[]{:S(2)}) async-start(), calls=%async_computation.15 | async-start | bytes 655360 | tf_op jit(solution)/shard_map/reduce_scatter | solution.py:195
  547.8 101.9 %all-reduce.11.cloned.1.call-start = ((), (), s32[]{:S(2)}) async-start(), calls=%async_computation.13 | async-start | bytes 8388608 | tf_op jit(solution)/shard_map/psum | solution.py:114
  553.1 99.0 %reduce-scatter.13.cloned.1.call-start = ((), (), s32[]{:S(2)}) async-start(), calls=%async_computation.16 | async-start | bytes 2621440 | tf_op jit(solution)/shard_map/reduce_scatter | solution.py:196
  561.7 119.4 %reduce-scatter.15.cloned.1.call-start = ((), (), s32[]{:S(2)}) async-start(), calls=%async_computation.17 | async-start | bytes 2621440 | tf_op jit(solution)/shard_map/reduce_scatter | solution.py:197
  569.9 34.1 %copy-start.24 = (f32[128,256]{1,0:T(8,128)S(1)}, f32[128,256]{1,0:T(8,128)}, u32[]{:S(2)}) copy-start(f32[128,256]{1,0:T(8,128)} %param.19) | copy-start | bytes 393220
  569.9 34.1 %copy-start.25 = (f32[2,128,256]{2,1,0:T(8,128)S(1)}, f32[2,128,256]{2,1,0:T(8,128)}, u32[]{:S(2)}) copy-start(f32[2,128,256]{2,1,0:T(8,128)} %param.25) | copy-start | bytes 786436
  570.0 82.1 %copy-start.17 = (f32[256,512]{1,0:T(8,128)S(1)}, f32[256,512]{1,0:T(8,128)}, u32[]{:S(2)}) copy-start(f32[256,512]{1,0:T(8,128)} %param.20) | copy-start | bytes 1572868
  570.0 145.1 %reduce-scatter.9.cloned.1.call-start = ((), (), s32[]{:S(2)}) async-start(), calls=%async_computation.14 | async-start | bytes 1966080 | tf_op jit(solution)/shard_map/reduce_scatter | solution.py:194
  575.3 105.9 %copy-start.19 = (f32[512,256]{1,0:T(8,128)S(1)}, f32[512,256]{1,0:T(8,128)}, u32[]{:S(2)}) copy-start(f32[512,256]{1,0:T(8,128)} %param.21) | copy-start | bytes 1572868
  575.8 139.3 %copy-start.15 = (f32[3,256,128]{1,2,0:T(8,128)S(1)}, f32[3,256,128]{1,2,0:T(8,128)}, u32[]{:S(2)}) copy-start(f32[3,256,128]{1,2,0:T(8,128)} %copy-done.14) | copy-start | bytes 1179652
  578.9 137.5 %copy-start.28 = (f32[2,96]{1,0:T(2,128)}, f32[2,96]{1,0:T(2,128)S(1)}, u32[]{:S(2)}) copy-start(f32[2,96]{1,0:T(2,128)S(1)} %copy.196) | copy-start | bytes 2308
  (25 other events, 159.1 us)
Sparse Core Ops, SparseCore 0:
  10.4 49.5 all-gather.5
  79.7 95.2 all-reduce.4
  196.8 96.5 all-reduce.6
  294.9 46.9 all-gather.11
  369.8 95.2 all-reduce.8
  553.2 96.5 all-reduce.10
Sparse Core Ops, SparseCore 1:
  82.4 25.2 all-gather.7
  109.9 26.2 all-gather.9
  522.6 24.3 reduce-scatter.18
  550.9 24.0 reduce-scatter.16
  578.9 25.0 reduce-scatter.10
  607.6 35.0 reduce-scatter.12
  646.1 35.1 reduce-scatter.14
  684.0 31.0 reduce-scatter.8
where the time goes:
time: 737 us; the launch traced here: 728 us
  waiting for transfers between devices  448 us (61%)
  matrix products  111 us (15%)
  other arithmetic  77.2 us (10%)
  blocking collectives  41.4 us (6%)
  local copies, waits for them, and re-layouts  32.2 us (4%)
  between operations  16.9 us (2%)
    psum x4, waiting for transfers between devices, reduce_rows(): return lax.psum(term.astype(jnp.bfloat16), 'tensor').astype(jnp.float32)  319 us
    all_gather x2, waiting for transfers between devices, spread(): return lax.all_gather(rows_b, 'tensor', axis=0, tiled=True)  49.6 us
    reduce_scatter x1, waiting for transfers between devices, on_device(): lax.psum_scatter(g_qkv, 'dp', scatter_dimension=1, tiled=True)  30.3 us
    reduce_scatter x1, waiting for transfers between devices, on_device(): lax.psum_scatter(g_reduce, 'dp', scatter_dimension=1, tiled=True)  25.3 us
    reduce_scatter x1, waiting for transfers between devices, on_device(): lax.psum_scatter(g_proj, 'dp', scatter_dimension=1, tiled=True)  22 us
    unnamed x84, local copies, waits for them, and re-layouts  17.6 us
    dot_general x1, matrix products, on_device(): jnp.einsum('shqk,skhe->sqhe', d_score, keys_h, preferred_element_type=sin...  16 us
    dot_general x1, matrix products, on_device(): jnp.einsum('shqk,sqhe->skhe', d_score, query_h, preferred_element_type=si...  15.8 us
  transfers between devices with their start and end apart: 14, of which 9 were waited for; matrix products, arithmetic and copies ran while one was open for 14% of the time, Pallas kernels for 0%

commit v1 on v0

--- a/solution.py
+++ b/solution.py
@@ -13,6 +13,12 @@
 learn_rate = 0.02
 decay_rate = 0.01
 adam_eps = 1e-08
+
+
+def gather_and_add(x, axis):
+    shards = lax.all_gather(x, axis, axis=0, tiled=False)
+    acc = shards.sum(axis=0)
+    return acc
 
 
 def layer_norm(resid, gain, shift):
@@ -111,7 +117,7 @@
     x_full = spread(block_in)
 
     def reduce_rows(term):
-        return lax.psum(term.astype(jnp.bfloat16), "tensor").astype(jnp.float32)
+        return gather_and_add(term.astype(jnp.bfloat16), "tensor").astype(jnp.float32)
 
     def own_rows(matrix):
         return lax.dynamic_slice_in_dim(matrix, first_row, share, 0)

time: 737 us -> 1590 us (2.16)
  waiting for transfers between devices: 448 us -> 1250 us
  other arithmetic: 77.2 us -> 136 us
    all_gather x0 -> x4, waiting for transfers between devices: none -> 1120 us  [gather_and_add(): shards = lax.all_gather(x, axis, axis=0, tiled=False)]
    psum x4 -> x0, waiting for transfers between devices: 319 us -> none  [reduce_rows(): return lax.psum(term.astype(jnp.bfloat16), 'tensor').astype(jnp.float32)]
    reduce_sum x0 -> x4, other arithmetic: none -> 57.8 us  [gather_and_add(): acc = shards.sum(axis=0)]
    reduce_scatter x1, waiting for transfers between devices: 25.3 us -> 0.01 us  [on_device(): lax.psum_scatter(g_reduce, 'dp', scatter_dimension=1, tiled=True)]
    all_gather x1, waiting for transfers between devices: 0.01 us -> 21.2 us  [on_device(): lax.all_gather(reduce_weight.astype(half), 'dp', axis=1, tiled=True)]
    all_gather x2, waiting for transfers between devices: 49.6 us -> 32.8 us  [spread(): return lax.all_gather(rows_b, 'tensor', axis=0, tiled=True)]
  transfers between devices with their start and end apart: 14 -> 14, of which waited for: 9 -> 11; matrix products, arithmetic and copies ran while one was open for 14% -> 13% of each run, Pallas kernels for 0% -> 0%
where the time goes in v1:
time: 1590 us; the launch traced here: 1580 us
  waiting for transfers between devices  1250 us (79%)
  other arithmetic  136 us (9%)
  matrix products  114 us (7%)
  blocking collectives  41 us (3%)
  local copies, waits for them, and re-layouts  31.7 us (2%)
    all_gather x4, waiting for transfers between devices, gather_and_add(): shards = lax.all_gather(x, axis, axis=0, tiled=False)  1120 us
    reduce_sum x4, other arithmetic, gather_and_add(): acc = shards.sum(axis=0)  57.8 us
    all_gather x2, waiting for transfers between devices, spread(): return lax.all_gather(rows_b, 'tensor', axis=0, tiled=True)  32.8 us
  transfers between devices with their start and end apart: 14, of which 11 were waited for; matrix products, arithmetic and copies ran while one was open for 13% of the time, Pallas kernels for 0%

profile of v1, /device:TPU:0, one launch (start us, length us, event | category | flops | bytes accessed | tf_op | source)
XLA Modules:
  0.0 1584.9 jit_solution(3031992312584449854)
XLA Ops:
  8.7 9.4 all-gather.4
  21.2 10.0 all_gather.51
  31.2 13.3 all_gather.49
  44.6 14.6 all-gather.14.cloned.1.call-done
  79.1 8.4 all_gather.54
  88.1 276.9 %all-gather.22.cloned.1.call-done = bf16[16384,1024]{1,0:T(8,128)(2,1)} async-done(((bf16[2048,1024]{1,0:T(8,128)(2,1)}), bf16[16384,1024]{1,0:T(8,128)(2,1)}) %all-gather.22.cloned.1.call-update) | async-done | bytes 33554448 | tf_op jit(solution)/shard_map/all_gather | solution.py:19
  365.0 14.4 reduce_sum.233
  399.6 21.2 %all-gather.18.cloned.1.call-done = bf16[512,1024]{1,0:T(8,128)(2,1)} async-done(((bf16[512,256]{1,0:T(8,128)(2,1)}), bf16[512,1024]{1,0:T(8,128)(2,1)}) %all-gather.18.cloned.1.call-update) | async-done | bytes 1048592 | tf_op jit(solution)/shard_map/all_gather | solution.py:101
  428.0 287.7 %all-gather.24.cloned.1.call-done = bf16[16384,1024]{1,0:T(8,128)(2,1)} async-done(((bf16[2048,1024]{1,0:T(8,128)(2,1)}), bf16[16384,1024]{1,0:T(8,128)(2,1)}) %all-gather.24.cloned.1.call-update) | async-done | bytes 33554448 | tf_op jit(solution)/shard_map/all_gather | solution.py:19
  715.7 14.8 reduce_sum.236
  744.1 18.2 %all-gather.20.cloned.1.call-done = bf16[2048,1024]{1,0:T(8,128)(2,1)} async-done(((bf16[256,1024]{1,0:T(8,128)(2,1)}), bf16[2048,1024]{1,0:T(8,128)(2,1)}) %all-gather.20.cloned.1.call-update) | async-done | bytes 4194320 | tf_op jit(solution)/shard_map/all_gather | solution.py:64
  762.2 11.6 multiply_reduce_fusion
  790.1 8.6 fusion.57
  798.8 9.4 fusion.37
  808.5 269.1 %all-gather.26.cloned.1.call-done = bf16[16384,1024]{1,0:T(8,128)(2,1)} async-done(((bf16[2048,1024]{1,0:T(8,128)(2,1)}), bf16[16384,1024]{1,0:T(8,128)(2,1)}) %all-gather.26.cloned.1.call-update) | async-done | bytes 33554448 | tf_op jit(solution)/shard_map/all_gather | solution.py:19
  1077.6 14.4 reduce_sum.241
  1092.1 12.2 multiply_reduce_fusion.1
  1126.4 16.5 %fusion.125 = (f32[2,64]{1,0:T(2,128)S(1)}, bf16[4,512,2,64]{1,3,2,0:T(8,128)(2,1)}) fusion(f32[4,2,512,512]{2,3,1,0:T(8,128)} %fusion.77, f32[4,2,512]{2,1,0:T(2,128)S(1)} %bitcast.230, f32[4,2,512,512]{2,3,1,0:T(8,128)} %copy-done.9, pred[4,512]{1,0:T(4,128)(4,1)S(1)} %fusion.96, bf16[4,512,2,64]{1,0,3,2:T(4,128)(2,1)S(1)} %copy-done.17), kind=kOutput, calls=%fused_computation.184 | convolution fusion | flops 292032896 | bytes 17844736 | tf_op jit(solution)/shard_map/shqk,skhe->sqhe/dot_general | solution.py:181
  1155.6 15.7 fusion.53
  1199.4 9.4 reduce-scatter.17.cloned.1.call-done
  1210.7 26.4 %reduce-scatter.11.cloned.1.call-done = f32[128,256]{1,0:T(8,128)} async-done(((f32[128,1024]{1,0:T(8,128)}), f32[128,256]{1,0:T(8,128)}) %reduce-scatter.11.cloned.1.call-update) | async-done | bytes 131088 | tf_op jit(solution)/shard_map/reduce_scatter | solution.py:201
  1239.6 31.7 %reduce-scatter.9.cloned.1.call-done = f32[3,256,128]{1,2,0:T(8,128)} async-done(((f32[3,1024,128]{1,2,0:T(8,128)}), f32[3,256,128]{1,2,0:T(8,128)}) %reduce-scatter.9.cloned.1.call-update) | async-done | bytes 393232 | tf_op jit(solution)/shard_map/reduce_scatter | solution.py:200
  1276.7 284.7 %all-gather.28.cloned.1.call-done = bf16[16384,1024]{1,0:T(8,128)(2,1)} async-done(((bf16[2048,1024]{1,0:T(8,128)(2,1)}), bf16[16384,1024]{1,0:T(8,128)(2,1)}) %all-gather.28.cloned.1.call-update) | async-done | bytes 33554448 | tf_op jit(solution)/shard_map/all_gather | solution.py:19
  1561.4 14.2 reduce_sum.245
  (202 shorter events, 157.0 us)
Async XLA Ops:
  7.2 52.0 %all-gather.14.cloned.1.call-start = ((), (), s32[]{:S(2)}) async-start(), calls=%async_computation.6 | async-start | bytes 4718592 | tf_op jit(solution)/shard_map/all_gather | solution.py:64
  7.9 357.0 %all-gather.22.cloned.1.call-start = ((), (), s32[]{:S(2)}) async-start(), calls=%async_computation.15 | async-start | bytes 37748736 | tf_op jit(solution)/shard_map/all_gather | solution.py:19
  20.1 43.4 %copy-start.15 = (f32[3,256,128]{1,2,0:T(8,128)}, f32[3,256,128]{1,2,0:T(8,128)S(1)}, u32[]{:S(2)}) copy-start(f32[3,256,128]{1,2,0:T(8,128)S(1)} %copy.154) | copy-start | bytes 1179652
  44.5 14.7 copy-start.24
  44.6 21.6 %copy-start.31 = (f32[2,64]{1,0:T(2,128)}, f32[2,64]{1,0:T(2,128)S(1)}, u32[]{:S(2)}) copy-start(f32[2,64]{1,0:T(2,128)S(1)} %get-tuple-element.167) | copy-start | bytes 1540
  77.4 314.7 %all-gather.16.cloned.1.call-start = ((), (), s32[]{:S(2)}) async-start(), calls=%async_computation.7 | async-start | bytes 1310720 | tf_op jit(solution)/shard_map/all_gather | solution.py:100
  78.2 342.5 %all-gather.18.cloned.1.call-start = ((), (), s32[]{:S(2)}) async-start(), calls=%async_computation.8 | async-start | bytes 1310720 | tf_op jit(solution)/shard_map/all_gather | solution.py:101
  79.0 636.7 %all-gather.24.cloned.1.call-start = ((), (), s32[]{:S(2)}) async-start(), calls=%async_computation.16 | async-start | bytes 37748736 | tf_op jit(solution)/shard_map/all_gather | solution.py:19
  426.9 335.3 %all-gather.20.cloned.1.call-start = ((), (), s32[]{:S(2)}) async-start(), calls=%async_computation.9 | async-start | bytes 4718592 | tf_op jit(solution)/shard_map/all_gather | solution.py:64
  427.5 650.1 %all-gather.26.cloned.1.call-start = ((), (), s32[]{:S(2)}) async-start(), calls=%async_computation.17 | async-start | bytes 37748736 | tf_op jit(solution)/shard_map/all_gather | solution.py:19
  790.0 399.4 %reduce-scatter.13.cloned.1.call-start = ((), (), s32[]{:S(2)}) async-start(), calls=%async_computation.12 | async-start | bytes 2621440 | tf_op jit(solution)/shard_map/reduce_scatter | solution.py:202
  798.8 394.3 %reduce-scatter.15.cloned.1.call-start = ((), (), s32[]{:S(2)}) async-start(), calls=%async_computation.13 | async-start | bytes 2621440 | tf_op jit(solution)/shard_map/reduce_scatter | solution.py:203
  808.3 388.4 %reduce-scatter.19.cloned.1.call-start = ((), (), s32[]{:S(2)}) async-start(), calls=%async_computation.19 | async-start | bytes 245760
  1126.4 16.5 %copy-start.22 = (bf16[4,512,2,64]{1,3,2,0:T(8,128)(2,1)S(1)}, bf16[4,512,2,64]{1,3,2,0:T(8,128)(2,1)}, u32[]{:S(2)}) copy-start(bf16[4,512,2,64]{1,3,2,0:T(8,128)(2,1)} %copy.162) | copy-start | bytes 1572868
  1149.8 59.0 %reduce-scatter.17.cloned.1.call-start = ((), (), s32[]{:S(2)}) async-start(), calls=%async_computation.14 | async-start | bytes 40960 | tf_op jit(solution)/shard_map/reduce_scatter | solution.py:205
  1155.5 15.8 copy-start.25
  1155.5 81.6 %reduce-scatter.11.cloned.1.call-start = ((), (), s32[]{:S(2)}) async-start(), calls=%async_computation.11 | async-start | bytes 655360 | tf_op jit(solution)/shard_map/reduce_scatter | solution.py:201
  1175.1 96.2 %reduce-scatter.9.cloned.1.call-start = ((), (), s32[]{:S(2)}) async-start(), calls=%async_computation.10 | async-start | bytes 1966080 | tf_op jit(solution)/shard_map/reduce_scatter | solution.py:200
  1180.6 380.8 %all-gather.28.cloned.1.call-start = ((), (), s32[]{:S(2)}) async-start(), calls=%async_computation.18 | async-start | bytes 37748736 | tf_op jit(solution)/shard_map/all_gather | solution.py:19
  1186.0 22.8 %copy-start.29 = (f32[6,256]{1,0:T(8,128)S(1)}, f32[6,256]{1,0:T(8,128)}, u32[]{:S(2)}) copy-start(f32[6,256]{1,0:T(8,128)} %param.23) | copy-start | bytes 18436
  1186.0 51.2 %copy-start.26 = (f32[128,256]{1,0:T(8,128)S(1)}, f32[128,256]{1,0:T(8,128)}, u32[]{:S(2)}) copy-start(f32[128,256]{1,0:T(8,128)} %param.19) | copy-start | bytes 393220
  1186.0 51.1 %copy-start.27 = (f32[2,128,256]{2,1,0:T(8,128)S(1)}, f32[2,128,256]{2,1,0:T(8,128)}, u32[]{:S(2)}) copy-start(f32[2,128,256]{2,1,0:T(8,128)} %param.25) | copy-start | bytes 786436
  1186.1 85.2 %copy-start.16 = (f32[3,256,128]{1,2,0:T(8,128)S(1)}, f32[3,256,128]{1,2,0:T(8,128)}, u32[]{:S(2)}) copy-start(f32[3,256,128]{1,2,0:T(8,128)} %copy-done.15) | copy-start | bytes 1179652
  1197.5 378.1 %copy-start.33 = (f32[2,96]{1,0:T(2,128)}, f32[2,96]{1,0:T(2,128)S(1)}, u32[]{:S(2)}) copy-start(f32[2,96]{1,0:T(2,128)S(1)} %copy.196) | copy-start | bytes 2308
  (28 other events, 199.9 us)
Sparse Core Ops, SparseCore 0:
  9.6 49.5 all-gather.13
  77.5 287.3 all-gather.21
  367.4 24.6 all-gather.15
  394.3 26.3 all-gather.17
  427.0 288.5 all-gather.23
  717.1 45.0 all-gather.19
  790.2 287.4 all-gather.25
  1081.2 33.3 reduce-scatter.12
  1118.1 35.1 reduce-scatter.14
  1156.5 24.2 reduce-scatter.18
  1184.7 24.0 reduce-scatter.16
  1212.0 25.0 reduce-scatter.10
  1240.1 31.0 reduce-scatter.8
  1272.7 288.6 all-gather.27
